TPU v7x, 32 devices: a whole 2x2x4 slice. The times are simulated.
32 devices in a mesh: gx: 4 (over y, x), gy: 4 (over z), gz: 2 (over core).
Axes of the slice: x: 2, y: 2, z: 4, core: 2. Of those that a mesh axis runs over, the one named last changes fastest.
Arguments:
- state: float32 [3, 32, 160, 512], P(None, 'gz', 'gy', 'gx'), may hold values from -6 to 6
- right_side: float32 [3, 32, 160, 512], P(None, 'gz', 'gy', 'gx'), may hold values from -6 to 6
- permeability: bfloat16 [32, 160, 512], P('gz', 'gy', 'gx'), may hold values from 0.099609375 to 10
- pore_volume: bfloat16 [32, 160, 512], P('gz', 'gy', 'gx'), may hold values from 0.019897461 to 0.19921875
- facies: int32 [32], P('gz'), may hold values from 0 to 3
- storage_table: float32 [4, 3, 3], replicated, may hold values from -0.3 to 2, as said below
- coupling_table: float32 [4, 3, 3], replicated, may hold values from -0.3 to 2, as said below
Outputs:
- new_state: float32 [3, 32, 160, 512], P(None, 'gz', 'gy', 'gx')
- correction: float32 [160, 512], P('gy', 'gx')
Inputs may be any that keep to these rules, and one draw needn't show every extreme that they name: `storage_table`: each facies block has a diagonal of 1 to 2 and off-diagonal entries of magnitude at most 0.3. `coupling_table`: each facies block has a diagonal of 1 to 2 and off-diagonal entries of magnitude at most 0.3.
All inputs are finite; a program needn't handle non-finite values.
Results may differ from a plain program's by a relative error of at most 0.0003.
Values sent between devices are 32-bit elements; how exact they have to be, the bound alone decides.
A program may use at most 64 MiB of HBM per device.

v0:
```python
import jax
import jax.numpy as jnp
from jax import lax
from jax.sharding import PartitionSpec as P

SWEEPS = 8
relax = 0.8


def extended(cells, sides, width):
    for axis, dim in sides:
        count = lax.axis_size(axis)
        ends = count - 1
        head = lax.slice_in_dim(cells, 0, width, axis=dim)
        tail = lax.slice_in_dim(cells, cells.shape[dim] - width, cells.shape[dim], axis=dim)
        cells = jnp.concatenate(
            [
                lax.ppermute(tail, axis, [(i, (i + 1) % count) for i in range(ends)]),
                cells,
                lax.ppermute(head, axis, [((i + 1) % count, i) for i in range(ends)]),
            ],
            axis=dim,
        )
    return cells


def layer_tables(facies, table):
    onehot = (facies[:, None] == jnp.arange(table.shape[0])[None, :]).astype(jnp.float32)
    return jnp.dot(onehot, table.reshape(table.shape[0], 9), precision=lax.Precision.HIGHEST)


def layer_coefficient(rows, row_index, column_index):
    return rows[:, 3 * row_index + column_index][:, None, None]


def neighbours(padded):
    return [
        padded[..., 2:, 1:-1, 1:-1],
        padded[..., :-2, 1:-1, 1:-1],
        padded[..., 1:-1, 2:, 1:-1],
        padded[..., 1:-1, :-2, 1:-1],
        padded[..., 1:-1, 1:-1, 2:],
        padded[..., 1:-1, 1:-1, :-2],
    ]


def face_weights(padded_perm):
    center = padded_perm[1:-1, 1:-1, 1:-1]
    return [2.0 * center * nearby / (center + nearby) for nearby in neighbours(padded_perm)]


def apply_operator(padded_state, weights, storage, storage_rows, coupling_rows):
    center = padded_state[:, 1:-1, 1:-1, 1:-1]
    fluxes = jnp.zeros_like(center)
    for weight, nearby in zip(weights, neighbours(padded_state)):
        fluxes = fluxes + weight[None] * (center - nearby)
    outputs = []
    for row_index in range(3):
        local = sum((layer_coefficient(storage_rows, row_index, k) * center[k] for k in range(3)))
        moved = sum((layer_coefficient(coupling_rows, row_index, k) * fluxes[k] for k in range(3)))
        outputs.append(storage * local + moved)
    return jnp.stack(outputs)


def coarse_planes(residual, weights, storage, storage_rows, coupling_rows):
    first_coupling = layer_coefficient(coupling_rows, 0, 0)
    first_storage = layer_coefficient(storage_rows, 0, 0)
    items = [residual[0], storage * first_storage] + [
        weights[k] * first_coupling for k in range(2, 6)
    ]
    return jnp.stack([jnp.sum(item, axis=0) for item in items])


def jacobi(field, bordered, planes):
    diagonal = planes[1] + planes[2] + planes[3] + planes[4] + planes[5]
    nearby = (
        planes[2] * bordered[2:, 1:-1]
        + planes[3] * bordered[:-2, 1:-1]
        + planes[4] * bordered[1:-1, 2:]
        + planes[5] * bordered[1:-1, :-2]
    )
    return field + relax * (planes[0] - diagonal * field + nearby) / diagonal


def column_image(correction, bordered, weights, storage, storage_rows, coupling_rows):
    areal = (
        weights[2] * (correction - bordered[2:, 1:-1])
        + weights[3] * (correction - bordered[:-2, 1:-1])
        + weights[4] * (correction - bordered[1:-1, 2:])
        + weights[5] * (correction - bordered[1:-1, :-2])
    )
    return jnp.stack(
        [
            storage * layer_coefficient(storage_rows, r, 0) * correction
            + layer_coefficient(coupling_rows, r, 0) * areal
            for r in range(3)
        ]
    )


def block_solve(weights, storage, storage_rows, coupling_rows, residual):
    face_total = weights[0] + weights[1] + weights[2] + weights[3] + weights[4] + weights[5]
    entries = [
        [
            storage * layer_coefficient(storage_rows, r, c)
            + face_total * layer_coefficient(coupling_rows, r, c)
            for c in range(3)
        ]
        for r in range(3)
    ]

    def cofactor(r, c):
        return (
            entries[(r + 1) % 3][(c + 1) % 3] * entries[(r + 2) % 3][(c + 2) % 3]
            - entries[(r + 1) % 3][(c + 2) % 3] * entries[(r + 2) % 3][(c + 1) % 3]
        )

    factors = [[cofactor(r, c) for c in range(3)] for r in range(3)]
    determinant = (
        entries[0][0] * factors[0][0]
        + entries[0][1] * factors[0][1]
        + entries[0][2] * factors[0][2]
    )
    return jnp.stack(
        [
            (
                factors[0][r] * residual[0]
                + factors[1][r] * residual[1]
                + factors[2][r] * residual[2]
            )
            / determinant
            for r in range(3)
        ]
    )


def per_device(state, right_side, permeability, pore_volume, facies, storage_table, coupling_table):
    perm_wide = permeability.astype(jnp.float32)
    storage = pore_volume.astype(jnp.float32)
    storage_rows = layer_tables(facies, storage_table)
    coupling_rows = layer_tables(facies, coupling_table)
    stacked = jnp.concatenate([state, perm_wide[None]], axis=0)
    padded = extended(stacked, (("gz", 1), ("gy", 2), ("gx", 3)), 1)
    weights = face_weights(padded[3])
    residual = right_side - apply_operator(
        padded[:3], weights, storage, storage_rows, coupling_rows
    )
    planes = coarse_planes(residual, weights, storage, storage_rows, coupling_rows)
    totals = lax.psum(planes, "gz")
    correction = jnp.zeros(totals.shape[1:], jnp.float32)
    for repeat_index in range(SWEEPS):
        bordered = extended(correction, (("gy", 0), ("gx", 1)), 1)
        correction = jacobi(correction, bordered, totals)
    state_one = state.at[0].add(correction[None])
    bordered = extended(correction, (("gy", 0), ("gx", 1)), 1)
    later_residual = residual - column_image(
        correction, bordered, weights, storage, storage_rows, coupling_rows
    )
    new_state = state_one + block_solve(
        weights, storage, storage_rows, coupling_rows, later_residual
    )
    return (new_state, correction)


def solution(mesh):
    return jax.shard_map(
        per_device,
        mesh=mesh,
        in_specs=(
            P(None, "gz", "gy", "gx"),
            P(None, "gz", "gy", "gx"),
            P("gz", "gy", "gx"),
            P("gz", "gy", "gx"),
            P("gz"),
            P(),
            P(),
        ),
        out_specs=(P(None, "gz", "gy", "gx"), P("gy", "gx")),
        check_vma=False,
    )
```

profile of v0, /device:TPU:28, one launch (start us, length us, event | category | flops | bytes accessed | tf_op | source)
XLA Modules:
  0.0 220.8 jit_solution(13019892907075081389)
XLA Ops:
  18.2 5.0 %collective-permute-start.3 = (f32[4,18,1,128]{3,0,2,1:T(4,128)S(1)}, f32[4,18,1,128]{3,0,2,1:T(4,128)S(1)}, u32[]{:S(2)}, u32[]{:S(2)}) collective-permute-start(f32[4,18,1,128]{3,0,2,1:T(4,128)S(1)} %copy.245), channel_id=1, source_target_pairs={{2,0},{4,2},{6,4},{3,1},{5,3},{7,5},{10,8},{12,10},{14,12},{11,9},... | collective-permute-start | bytes 110600 | tf_op jit(solution)/shard_map/ppermute | solution.py:20
  29.1 3.4 %collective-permute-start.4 = (f32[4,18,42,1]{2,0,3,1:T(4,128)S(1)}, f32[4,18,42,1]{2,0,3,1:T(4,128)S(1)}, u32[]{:S(2)}, u32[]{:S(2)}) collective-permute-start(f32[4,18,42,1]{2,0,3,1:T(4,128)S(1)} %copy.218), channel_id=1, source_target_pairs={{0,8},{8,16},{16,24},{1,9},{9,17},{17,25},{2,10},{10,18},{18,26},{... | collective-permute-start | bytes 36296 | tf_op jit(solution)/shard_map/ppermute | solution.py:18
  33.2 3.3 %collective-permute-start.5 = (f32[4,18,42,1]{2,0,3,1:T(4,128)S(1)}, f32[4,18,42,1]{2,0,3,1:T(4,128)S(1)}, u32[]{:S(2)}, u32[]{:S(2)}) collective-permute-start(f32[4,18,42,1]{2,0,3,1:T(4,128)S(1)} %copy.219), channel_id=1, source_target_pairs={{8,0},{16,8},{24,16},{9,1},{17,9},{25,17},{10,2},{18,10},{26,18},{... | collective-permute-start | bytes 36296 | tf_op jit(solution)/shard_map/ppermute | solution.py:20
  44.0 3.3 %fusion.2 = f32[3,16,40,128]{3,2,1,0:T(8,128)S(1)} fusion(f32[3,16,40,128]{3,2,1,0:T(8,128)S(1)} %copy.254, f32[4,18,42,1]{3,2,1,0:T(8,128)S(1)} %copy.220, f32[4,18,1,128]{3,2,1,0:T(1,128)S(1)} %copy.217, f32[4,18,1,128]{3,2,1,0:T(1,128)S(1)} %copy.216, f32[4,1,40,128]{3,2,1,0:T(8,128)S(1)} %collective-permute-done.1, ...), kind=kLoop, calls=%fused_computation.18 | loop fusion | flops 10076160 | bytes 4521600 | tf_op jit(solution)/shard_map/add | solution.py:56
  51.7 4.2 %collective-permute-start.8 = (f32[42,1]{1,0:T(8,128)S(1)}, f32[42,1]{1,0:T(8,128)S(1)}, u32[]{:S(2)}, u32[]{:S(2)}) collective-permute-start(f32[42,1]{1,0:T(8,128)S(1)} %get-tuple-element.66), channel_id=1, source_target_pairs={{8,0},{16,8},{24,16},{9,1},{17,9},{25,17},{10,2},{18,10},{26,18},{... | collective-permute-start | bytes 512 | tf_op jit(solution)/shard_map/ppermute | solution.py:20
  57.9 4.7 %collective-permute-done.9 = f32[42,1]{1,0:T(8,128)S(1)} collective-permute-done((f32[42,1]{1,0:T(8,128)S(1)}, f32[42,1]{1,0:T(8,128)S(1)}, u32[]{:S(2)}, u32[]{:S(2)}) %collective-permute-start.9) | collective-permute-done | bytes 200 | tf_op jit(solution)/shard_map/ppermute | solution.py:18
  62.6 9.7 %all-reduce.4.cloned.1.call-done = f32[6,40,128]{2,1,0:T(8,128)} async-done(((f32[6,40,128]{2,1,0:T(8,128)}), f32[6,40,128]{2,1,0:T(8,128)}) %all-reduce.4.cloned.1.call-update) | async-done | bytes 122896 | tf_op jit(solution)/shard_map/psum | solution.py:149
  77.2 4.2 %collective-permute-done.11 = f32[1,128]{1,0:T(1,128)S(1)} collective-permute-done((f32[1,128]{1,0:T(1,128)S(1)}, f32[1,128]{1,0:T(1,128)S(1)}, u32[]{:S(2)}, u32[]{:S(2)}) %collective-permute-start.11) | collective-permute-done | bytes 544 | tf_op jit(solution)/shard_map/ppermute | solution.py:18
  81.4 3.4 %collective-permute-start.12 = (f32[42,1]{1,0:T(8,128)S(1)}, f32[42,1]{1,0:T(8,128)S(1)}, u32[]{:S(2)}, u32[]{:S(2)}) collective-permute-start(f32[42,1]{1,0:T(8,128)S(1)} %get-tuple-element.64), channel_id=1, source_target_pairs={{8,0},{16,8},{24,16},{9,1},{17,9},{25,17},{10,2},{18,10},{26,18},{... | collective-permute-start | bytes 512 | tf_op jit(solution)/shard_map/ppermute | solution.py:20
  87.3 4.1 %collective-permute-done.13 = f32[42,1]{1,0:T(8,128)S(1)} collective-permute-done((f32[42,1]{1,0:T(8,128)S(1)}, f32[42,1]{1,0:T(8,128)S(1)}, u32[]{:S(2)}, u32[]{:S(2)}) %collective-permute-start.13) | collective-permute-done | bytes 200 | tf_op jit(solution)/shard_map/ppermute | solution.py:18
  96.1 4.2 %collective-permute-done.15 = f32[1,128]{1,0:T(1,128)S(1)} collective-permute-done((f32[1,128]{1,0:T(1,128)S(1)}, f32[1,128]{1,0:T(1,128)S(1)}, u32[]{:S(2)}, u32[]{:S(2)}) %collective-permute-start.15) | collective-permute-done | bytes 544 | tf_op jit(solution)/shard_map/ppermute | solution.py:18
  102.3 3.9 %collective-permute-start.17 = (f32[42,1]{1,0:T(8,128)S(1)}, f32[42,1]{1,0:T(8,128)S(1)}, u32[]{:S(2)}, u32[]{:S(2)}) collective-permute-start(f32[42,1]{1,0:T(8,128)S(1)} %get-tuple-element.63), channel_id=1, source_target_pairs={{0,8},{8,16},{16,24},{1,9},{9,17},{17,25},{2,10},{10,18},{18,26},{... | collective-permute-start | bytes 512 | tf_op jit(solution)/shard_map/ppermute | solution.py:18
  113.6 4.2 %collective-permute-done.19 = f32[1,128]{1,0:T(1,128)S(1)} collective-permute-done((f32[1,128]{1,0:T(1,128)S(1)}, f32[1,128]{1,0:T(1,128)S(1)}, u32[]{:S(2)}, u32[]{:S(2)}) %collective-permute-start.19) | collective-permute-done | bytes 544 | tf_op jit(solution)/shard_map/ppermute | solution.py:18
  119.7 3.9 %collective-permute-start.21 = (f32[42,1]{1,0:T(8,128)S(1)}, f32[42,1]{1,0:T(8,128)S(1)}, u32[]{:S(2)}, u32[]{:S(2)}) collective-permute-start(f32[42,1]{1,0:T(8,128)S(1)} %get-tuple-element.61), channel_id=1, source_target_pairs={{0,8},{8,16},{16,24},{1,9},{9,17},{17,25},{2,10},{10,18},{18,26},{... | collective-permute-start | bytes 512 | tf_op jit(solution)/shard_map/ppermute | solution.py:18
  130.5 4.2 %collective-permute-done.23 = f32[1,128]{1,0:T(1,128)S(1)} collective-permute-done((f32[1,128]{1,0:T(1,128)S(1)}, f32[1,128]{1,0:T(1,128)S(1)}, u32[]{:S(2)}, u32[]{:S(2)}) %collective-permute-start.23) | collective-permute-done | bytes 544 | tf_op jit(solution)/shard_map/ppermute | solution.py:18
  136.7 3.9 %collective-permute-start.25 = (f32[42,1]{1,0:T(8,128)S(1)}, f32[42,1]{1,0:T(8,128)S(1)}, u32[]{:S(2)}, u32[]{:S(2)}) collective-permute-start(f32[42,1]{1,0:T(8,128)S(1)} %get-tuple-element.59), channel_id=1, source_target_pairs={{0,8},{8,16},{16,24},{1,9},{9,17},{17,25},{2,10},{10,18},{18,26},{... | collective-permute-start | bytes 512 | tf_op jit(solution)/shard_map/ppermute | solution.py:18
  147.5 4.2 %collective-permute-done.27 = f32[1,128]{1,0:T(1,128)S(1)} collective-permute-done((f32[1,128]{1,0:T(1,128)S(1)}, f32[1,128]{1,0:T(1,128)S(1)}, u32[]{:S(2)}, u32[]{:S(2)}) %collective-permute-start.27) | collective-permute-done | bytes 544 | tf_op jit(solution)/shard_map/ppermute | solution.py:18
  153.6 3.9 %collective-permute-start.29 = (f32[42,1]{1,0:T(8,128)S(1)}, f32[42,1]{1,0:T(8,128)S(1)}, u32[]{:S(2)}, u32[]{:S(2)}) collective-permute-start(f32[42,1]{1,0:T(8,128)S(1)} %get-tuple-element.57), channel_id=1, source_target_pairs={{0,8},{8,16},{16,24},{1,9},{9,17},{17,25},{2,10},{10,18},{18,26},{... | collective-permute-start | bytes 512 | tf_op jit(solution)/shard_map/ppermute | solution.py:18
  163.6 4.2 %collective-permute-done.31 = f32[1,128]{1,0:T(1,128)S(1)} collective-permute-done((f32[1,128]{1,0:T(1,128)S(1)}, f32[1,128]{1,0:T(1,128)S(1)}, u32[]{:S(2)}, u32[]{:S(2)}) %collective-permute-start.31) | collective-permute-done | bytes 544 | tf_op jit(solution)/shard_map/ppermute | solution.py:18
  169.7 3.9 %collective-permute-start.33 = (f32[42,1]{1,0:T(8,128)S(1)}, f32[42,1]{1,0:T(8,128)S(1)}, u32[]{:S(2)}, u32[]{:S(2)}) collective-permute-start(f32[42,1]{1,0:T(8,128)S(1)} %get-tuple-element.55), channel_id=1, source_target_pairs={{0,8},{8,16},{16,24},{1,9},{9,17},{17,25},{2,10},{10,18},{18,26},{... | collective-permute-start | bytes 512 | tf_op jit(solution)/shard_map/ppermute | solution.py:18
  179.9 4.2 %collective-permute-done.35 = f32[1,128]{1,0:T(1,128)S(1)} collective-permute-done((f32[1,128]{1,0:T(1,128)S(1)}, f32[1,128]{1,0:T(1,128)S(1)}, u32[]{:S(2)}, u32[]{:S(2)}) %collective-permute-start.35) | collective-permute-done | bytes 544 | tf_op jit(solution)/shard_map/ppermute | solution.py:18
  186.1 3.9 %collective-permute-start.37 = (f32[42,1]{1,0:T(8,128)S(1)}, f32[42,1]{1,0:T(8,128)S(1)}, u32[]{:S(2)}, u32[]{:S(2)}) collective-permute-start(f32[42,1]{1,0:T(8,128)S(1)} %get-tuple-element.53), channel_id=1, source_target_pairs={{0,8},{8,16},{16,24},{1,9},{9,17},{17,25},{2,10},{10,18},{18,26},{... | collective-permute-start | bytes 512 | tf_op jit(solution)/shard_map/ppermute | solution.py:18
  196.0 4.2 %collective-permute-done.39 = f32[1,128]{1,0:T(1,128)S(1)} collective-permute-done((f32[1,128]{1,0:T(1,128)S(1)}, f32[1,128]{1,0:T(1,128)S(1)}, u32[]{:S(2)}, u32[]{:S(2)}) %collective-permute-start.39) | collective-permute-done | bytes 544 | tf_op jit(solution)/shard_map/ppermute | solution.py:18
  202.2 4.1 %collective-permute-start.41 = (f32[42,1]{1,0:T(8,128)S(1)}, f32[42,1]{1,0:T(8,128)S(1)}, u32[]{:S(2)}, u32[]{:S(2)}) collective-permute-start(f32[42,1]{1,0:T(8,128)S(1)} %get-tuple-element.51), channel_id=1, source_target_pairs={{0,8},{8,16},{16,24},{1,9},{9,17},{17,25},{2,10},{10,18},{18,26},{... | collective-permute-start | bytes 512 | tf_op jit(solution)/shard_map/ppermute | solution.py:18
  (256 shorter events, 103.4 us)
Async XLA Ops:
  7.2 65.1 %all-reduce.4.cloned.1.call-start = ((), (), s32[]{:S(2)}) async-start(), calls=%async_computation | async-start | bytes 245760 | tf_op jit(solution)/shard_map/psum | solution.py:149
  8.5 28.1 %collective-permute-start.6 = (f32[1,128]{1,0:T(1,128)S(1)}, f32[1,128]{1,0:T(1,128)S(1)}, u32[]{:S(2)}, u32[]{:S(2)}) collective-permute-start(f32[1,128]{1,0:T(1,128)S(1)} %broadcast.60), channel_id=1, source_target_pairs={{2,0},{4,2},{6,4},{3,1},{5,3},{7,5},{10,8},{12,10},{14,12},{11,9},... | collective-permute-start | bytes 1544 | tf_op jit(solution)/shard_map/ppermute | solution.py:20
  10.8 25.7 %collective-permute-start.7 = (f32[1,128]{1,0:T(1,128)S(1)}, f32[1,128]{1,0:T(1,128)S(1)}, u32[]{:S(2)}, u32[]{:S(2)}) collective-permute-start(f32[1,128]{1,0:T(1,128)S(1)} %broadcast.60), channel_id=1, source_target_pairs={{0,2},{2,4},{4,6},{1,3},{3,5},{5,7},{8,10},{10,12},{12,14},{9,11},... | collective-permute-start | bytes 1544 | tf_op jit(solution)/shard_map/ppermute | solution.py:18
  16.9 6.9 %collective-permute-start.2 = (f32[4,18,1,128]{3,0,2,1:T(4,128)S(1)}, f32[4,18,1,128]{3,0,2,1:T(4,128)S(1)}, u32[]{:S(2)}, u32[]{:S(2)}) collective-permute-start(f32[4,18,1,128]{3,0,2,1:T(4,128)S(1)} %copy.244), channel_id=1, source_target_pairs={{0,2},{2,4},{4,6},{1,3},{3,5},{5,7},{8,10},{10,12},{12,14},{9,11},... | collective-permute-start | bytes 110600 | tf_op jit(solution)/shard_map/ppermute | solution.py:18
  18.2 6.6 %collective-permute-start.3 = (f32[4,18,1,128]{3,0,2,1:T(4,128)S(1)}, f32[4,18,1,128]{3,0,2,1:T(4,128)S(1)}, u32[]{:S(2)}, u32[]{:S(2)}) collective-permute-start(f32[4,18,1,128]{3,0,2,1:T(4,128)S(1)} %copy.245), channel_id=1, source_target_pairs={{2,0},{4,2},{6,4},{3,1},{5,3},{7,5},{10,8},{12,10},{14,12},{11,9},... | collective-permute-start | bytes 110600 | tf_op jit(solution)/shard_map/ppermute | solution.py:20
  29.1 7.5 %collective-permute-start.4 = (f32[4,18,42,1]{2,0,3,1:T(4,128)S(1)}, f32[4,18,42,1]{2,0,3,1:T(4,128)S(1)}, u32[]{:S(2)}, u32[]{:S(2)}) collective-permute-start(f32[4,18,42,1]{2,0,3,1:T(4,128)S(1)} %copy.218), channel_id=1, source_target_pairs={{0,8},{8,16},{16,24},{1,9},{9,17},{17,25},{2,10},{10,18},{18,26},{... | collective-permute-start | bytes 36296 | tf_op jit(solution)/shard_map/ppermute | solution.py:18
  51.7 6.2 %collective-permute-start.8 = (f32[42,1]{1,0:T(8,128)S(1)}, f32[42,1]{1,0:T(8,128)S(1)}, u32[]{:S(2)}, u32[]{:S(2)}) collective-permute-start(f32[42,1]{1,0:T(8,128)S(1)} %get-tuple-element.66), channel_id=1, source_target_pairs={{8,0},{16,8},{24,16},{9,1},{17,9},{25,17},{10,2},{18,10},{26,18},{... | collective-permute-start | bytes 512 | tf_op jit(solution)/shard_map/ppermute | solution.py:20
  56.0 6.6 %collective-permute-start.9 = (f32[42,1]{1,0:T(8,128)S(1)}, f32[42,1]{1,0:T(8,128)S(1)}, u32[]{:S(2)}, u32[]{:S(2)}) collective-permute-start(f32[42,1]{1,0:T(8,128)S(1)} %get-tuple-element.67), channel_id=1, source_target_pairs={{0,8},{8,16},{16,24},{1,9},{9,17},{17,25},{2,10},{10,18},{18,26},{... | collective-permute-start | bytes 512 | tf_op jit(solution)/shard_map/ppermute | solution.py:18
  81.4 5.8 %collective-permute-start.12 = (f32[42,1]{1,0:T(8,128)S(1)}, f32[42,1]{1,0:T(8,128)S(1)}, u32[]{:S(2)}, u32[]{:S(2)}) collective-permute-start(f32[42,1]{1,0:T(8,128)S(1)} %get-tuple-element.64), channel_id=1, source_target_pairs={{8,0},{16,8},{24,16},{9,1},{17,9},{25,17},{10,2},{18,10},{26,18},{... | collective-permute-start | bytes 512 | tf_op jit(solution)/shard_map/ppermute | solution.py:20
  84.8 6.6 %collective-permute-start.13 = (f32[42,1]{1,0:T(8,128)S(1)}, f32[42,1]{1,0:T(8,128)S(1)}, u32[]{:S(2)}, u32[]{:S(2)}) collective-permute-start(f32[42,1]{1,0:T(8,128)S(1)} %get-tuple-element.65), channel_id=1, source_target_pairs={{0,8},{8,16},{16,24},{1,9},{9,17},{17,25},{2,10},{10,18},{18,26},{... | collective-permute-start | bytes 512 | tf_op jit(solution)/shard_map/ppermute | solution.py:18
  100.4 5.8 %collective-permute-start.16 = (f32[42,1]{1,0:T(8,128)S(1)}, f32[42,1]{1,0:T(8,128)S(1)}, u32[]{:S(2)}, u32[]{:S(2)}) collective-permute-start(f32[42,1]{1,0:T(8,128)S(1)} %get-tuple-element.62), channel_id=1, source_target_pairs={{8,0},{16,8},{24,16},{9,1},{17,9},{25,17},{10,2},{18,10},{26,18},{... | collective-permute-start | bytes 512 | tf_op jit(solution)/shard_map/ppermute | solution.py:20
  102.3 6.6 %collective-permute-start.17 = (f32[42,1]{1,0:T(8,128)S(1)}, f32[42,1]{1,0:T(8,128)S(1)}, u32[]{:S(2)}, u32[]{:S(2)}) collective-permute-start(f32[42,1]{1,0:T(8,128)S(1)} %get-tuple-element.63), channel_id=1, source_target_pairs={{0,8},{8,16},{16,24},{1,9},{9,17},{17,25},{2,10},{10,18},{18,26},{... | collective-permute-start | bytes 512 | tf_op jit(solution)/shard_map/ppermute | solution.py:18
  117.8 5.8 %collective-permute-start.20 = (f32[42,1]{1,0:T(8,128)S(1)}, f32[42,1]{1,0:T(8,128)S(1)}, u32[]{:S(2)}, u32[]{:S(2)}) collective-permute-start(f32[42,1]{1,0:T(8,128)S(1)} %get-tuple-element.60), channel_id=1, source_target_pairs={{8,0},{16,8},{24,16},{9,1},{17,9},{25,17},{10,2},{18,10},{26,18},{... | collective-permute-start | bytes 512 | tf_op jit(solution)/shard_map/ppermute | solution.py:20
  119.7 6.6 %collective-permute-start.21 = (f32[42,1]{1,0:T(8,128)S(1)}, f32[42,1]{1,0:T(8,128)S(1)}, u32[]{:S(2)}, u32[]{:S(2)}) collective-permute-start(f32[42,1]{1,0:T(8,128)S(1)} %get-tuple-element.61), channel_id=1, source_target_pairs={{0,8},{8,16},{16,24},{1,9},{9,17},{17,25},{2,10},{10,18},{18,26},{... | collective-permute-start | bytes 512 | tf_op jit(solution)/shard_map/ppermute | solution.py:18
  134.8 5.8 %collective-permute-start.24 = (f32[42,1]{1,0:T(8,128)S(1)}, f32[42,1]{1,0:T(8,128)S(1)}, u32[]{:S(2)}, u32[]{:S(2)}) collective-permute-start(f32[42,1]{1,0:T(8,128)S(1)} %get-tuple-element.58), channel_id=1, source_target_pairs={{8,0},{16,8},{24,16},{9,1},{17,9},{25,17},{10,2},{18,10},{26,18},{... | collective-permute-start | bytes 512 | tf_op jit(solution)/shard_map/ppermute | solution.py:20
  136.7 6.6 %collective-permute-start.25 = (f32[42,1]{1,0:T(8,128)S(1)}, f32[42,1]{1,0:T(8,128)S(1)}, u32[]{:S(2)}, u32[]{:S(2)}) collective-permute-start(f32[42,1]{1,0:T(8,128)S(1)} %get-tuple-element.59), channel_id=1, source_target_pairs={{0,8},{8,16},{16,24},{1,9},{9,17},{17,25},{2,10},{10,18},{18,26},{... | collective-permute-start | bytes 512 | tf_op jit(solution)/shard_map/ppermute | solution.py:18
  151.7 5.8 %collective-permute-start.28 = (f32[42,1]{1,0:T(8,128)S(1)}, f32[42,1]{1,0:T(8,128)S(1)}, u32[]{:S(2)}, u32[]{:S(2)}) collective-permute-start(f32[42,1]{1,0:T(8,128)S(1)} %get-tuple-element.56), channel_id=1, source_target_pairs={{8,0},{16,8},{24,16},{9,1},{17,9},{25,17},{10,2},{18,10},{26,18},{... | collective-permute-start | bytes 512 | tf_op jit(solution)/shard_map/ppermute | solution.py:20
  153.6 6.6 %collective-permute-start.29 = (f32[42,1]{1,0:T(8,128)S(1)}, f32[42,1]{1,0:T(8,128)S(1)}, u32[]{:S(2)}, u32[]{:S(2)}) collective-permute-start(f32[42,1]{1,0:T(8,128)S(1)} %get-tuple-element.57), channel_id=1, source_target_pairs={{0,8},{8,16},{16,24},{1,9},{9,17},{17,25},{2,10},{10,18},{18,26},{... | collective-permute-start | bytes 512 | tf_op jit(solution)/shard_map/ppermute | solution.py:18
  167.8 5.8 %collective-permute-start.32 = (f32[42,1]{1,0:T(8,128)S(1)}, f32[42,1]{1,0:T(8,128)S(1)}, u32[]{:S(2)}, u32[]{:S(2)}) collective-permute-start(f32[42,1]{1,0:T(8,128)S(1)} %get-tuple-element.54), channel_id=1, source_target_pairs={{8,0},{16,8},{24,16},{9,1},{17,9},{25,17},{10,2},{18,10},{26,18},{... | collective-permute-start | bytes 512 | tf_op jit(solution)/shard_map/ppermute | solution.py:20
  169.7 6.7 %collective-permute-start.33 = (f32[42,1]{1,0:T(8,128)S(1)}, f32[42,1]{1,0:T(8,128)S(1)}, u32[]{:S(2)}, u32[]{:S(2)}) collective-permute-start(f32[42,1]{1,0:T(8,128)S(1)} %get-tuple-element.55), channel_id=1, source_target_pairs={{0,8},{8,16},{16,24},{1,9},{9,17},{17,25},{2,10},{10,18},{18,26},{... | collective-permute-start | bytes 512 | tf_op jit(solution)/shard_map/ppermute | solution.py:18
  184.1 5.8 %collective-permute-start.36 = (f32[42,1]{1,0:T(8,128)S(1)}, f32[42,1]{1,0:T(8,128)S(1)}, u32[]{:S(2)}, u32[]{:S(2)}) collective-permute-start(f32[42,1]{1,0:T(8,128)S(1)} %get-tuple-element.52), channel_id=1, source_target_pairs={{8,0},{16,8},{24,16},{9,1},{17,9},{25,17},{10,2},{18,10},{26,18},{... | collective-permute-start | bytes 512 | tf_op jit(solution)/shard_map/ppermute | solution.py:20
  186.1 6.6 %collective-permute-start.37 = (f32[42,1]{1,0:T(8,128)S(1)}, f32[42,1]{1,0:T(8,128)S(1)}, u32[]{:S(2)}, u32[]{:S(2)}) collective-permute-start(f32[42,1]{1,0:T(8,128)S(1)} %get-tuple-element.53), channel_id=1, source_target_pairs={{0,8},{8,16},{16,24},{1,9},{9,17},{17,25},{2,10},{10,18},{18,26},{... | collective-permute-start | bytes 512 | tf_op jit(solution)/shard_map/ppermute | solution.py:18
  200.3 6.1 %collective-permute-start.40 = (f32[42,1]{1,0:T(8,128)S(1)}, f32[42,1]{1,0:T(8,128)S(1)}, u32[]{:S(2)}, u32[]{:S(2)}) collective-permute-start(f32[42,1]{1,0:T(8,128)S(1)} %get-tuple-element.50), channel_id=1, source_target_pairs={{8,0},{16,8},{24,16},{9,1},{17,9},{25,17},{10,2},{18,10},{26,18},{... | collective-permute-start | bytes 512 | tf_op jit(solution)/shard_map/ppermute | solution.py:20
  202.2 6.6 %collective-permute-start.41 = (f32[42,1]{1,0:T(8,128)S(1)}, f32[42,1]{1,0:T(8,128)S(1)}, u32[]{:S(2)}, u32[]{:S(2)}) collective-permute-start(f32[42,1]{1,0:T(8,128)S(1)} %get-tuple-element.51), channel_id=1, source_target_pairs={{0,8},{8,16},{16,24},{1,9},{9,17},{17,25},{2,10},{10,18},{18,26},{... | collective-permute-start | bytes 512 | tf_op jit(solution)/shard_map/ppermute | solution.py:18
  (69 other events, 1000.4 us)
Sparse Core Ops, SparseCore 0:
  51.8 20.4 all-reduce.3
where the time goes:
time: 223 us; the launch traced here: 221 us
  starting transfers between devices  100 us (45%)
  waiting for transfers between devices  73.7 us (33%)
  other arithmetic  16.3 us (7%)
  between operations  15.4 us (7%)
  local copies, waits for them, and re-layouts  15.1 us (7%)
    ppermute x21, waiting for transfers between devices, extended(): lax.ppermute(tail, axis, [(i, (i + 1) % count) for i in range(ends)])  60.6 us
    ppermute x21, starting transfers between devices, extended(): lax.ppermute(head, axis, [((i + 1) % count, i) for i in range(ends)])  50 us
    ppermute x21, starting transfers between devices, extended(): lax.ppermute(tail, axis, [(i, (i + 1) % count) for i in range(ends)])  49.9 us
    psum x1, waiting for transfers between devices, per_device(): totals = lax.psum(planes, 'gz')  9.72 us
    unnamed x116, local copies, waits for them, and re-layouts  5.28 us
  transfers between devices with their start and end apart: 43, of which 21 were waited for; matrix products, arithmetic and copies ran while one was open for 4% of the time, Pallas kernels for 0%

commit v1 on v0

--- a/solution.py
+++ b/solution.py
@@ -146,7 +146,7 @@
         padded[:3], weights, storage, storage_rows, coupling_rows
     )
     planes = coarse_planes(residual, weights, storage, storage_rows, coupling_rows)
-    totals = lax.psum(planes, "gz")
+    totals = jnp.sum(lax.all_gather(planes, "gz"), axis=0)
     correction = jnp.zeros(totals.shape[1:], jnp.float32)
     for repeat_index in range(SWEEPS):
         bordered = extended(correction, (("gy", 0), ("gx", 1)), 1)

time: 223 us -> 198 us (0.89)
  waiting for transfers between devices: 73.7 us -> 57 us
  between operations: 15.4 us -> 2.1 us
  starting transfers between devices: 100 us -> 104 us
  other arithmetic: 16.3 us -> 12.9 us
  local copies, waits for them, and re-layouts: 15.1 us -> 18.5 us
    psum x1 -> x0, waiting for transfers between devices: 9.72 us -> none  [per_device(): totals = lax.psum(planes, 'gz')]
    ppermute x21, waiting for transfers between devices: 60.6 us -> 55.3 us  [extended(): lax.ppermute(tail, axis, [(i, (i + 1) % count) for i in range(ends)])]
    add x7, other arithmetic: 3.91 us -> 0.65 us  [jacobi(): return field + relax * (planes[0] - diagonal * field + nearby) / diagonal]
    ppermute x21, starting transfers between devices: 49.9 us -> 52.6 us  [extended(): lax.ppermute(tail, axis, [(i, (i + 1) % count) for i in range(ends)])]
    unnamed x116 -> x126, local copies, waits for them, and re-layouts: 5.28 us -> 7.41 us
  transfers between devices with their start and end apart: 43 -> 42, of which waited for: 21 -> 17; matrix products, arithmetic and copies ran while one was open for 4% -> 9% of each run, Pallas kernels for 0% -> 0%
where the time goes in v1:
time: 198 us; the launch traced here: 197 us
  starting transfers between devices  104 us (53%)
  waiting for transfers between devices  57 us (29%)
  local copies, waits for them, and re-layouts  18.5 us (9%)
  other arithmetic  12.9 us (7%)
  blocking collectives  2.18 us (1%)
  between operations  2.1 us (1%)
    ppermute x21, waiting for transfers between devices, extended(): lax.ppermute(tail, axis, [(i, (i + 1) % count) for i in range(ends)])  55.3 us
    ppermute x21, starting transfers between devices, extended(): lax.ppermute(tail, axis, [(i, (i + 1) % count) for i in range(ends)])  52.6 us
    ppermute x21, starting transfers between devices, extended(): lax.ppermute(head, axis, [((i + 1) % count, i) for i in range(ends)])  51.2 us
    unnamed x126, local copies, waits for them, and re-layouts  7.41 us
  transfers between devices with their start and end apart: 42, of which 17 were waited for; matrix products, arithmetic and copies ran while one was open for 9% of the time, Pallas kernels for 0%

profile of v1, /device:TPU:28, one launch (start us, length us, event | category | flops | bytes accessed | tf_op | source)
XLA Modules:
  0.0 196.8 jit_solution(7702420557982893749)
XLA Ops:
  11.7 5.0 %collective-permute-start.3 = (f32[4,18,1,128]{3,0,2,1:T(4,128)S(1)}, f32[4,18,1,128]{3,0,2,1:T(4,128)S(1)}, u32[]{:S(2)}, u32[]{:S(2)}) collective-permute-start(f32[4,18,1,128]{3,0,2,1:T(4,128)S(1)} %copy.239), channel_id=1, source_target_pairs={{2,0},{4,2},{6,4},{3,1},{5,3},{7,5},{10,8},{12,10},{14,12},{11,9},... | collective-permute-start | bytes 110600 | tf_op jit(solution)/shard_map/ppermute | solution.py:20
  22.6 3.4 %collective-permute-start.4 = (f32[4,18,42,1]{2,0,3,1:T(4,128)S(1)}, f32[4,18,42,1]{2,0,3,1:T(4,128)S(1)}, u32[]{:S(2)}, u32[]{:S(2)}) collective-permute-start(f32[4,18,42,1]{2,0,3,1:T(4,128)S(1)} %copy.212), channel_id=1, source_target_pairs={{0,8},{8,16},{16,24},{1,9},{9,17},{17,25},{2,10},{10,18},{18,26},{... | collective-permute-start | bytes 36296 | tf_op jit(solution)/shard_map/ppermute | solution.py:18
  26.8 3.3 %collective-permute-start.5 = (f32[4,18,42,1]{2,0,3,1:T(4,128)S(1)}, f32[4,18,42,1]{2,0,3,1:T(4,128)S(1)}, u32[]{:S(2)}, u32[]{:S(2)}) collective-permute-start(f32[4,18,42,1]{2,0,3,1:T(4,128)S(1)} %copy.213), channel_id=1, source_target_pairs={{8,0},{16,8},{24,16},{9,1},{17,9},{25,17},{10,2},{18,10},{26,18},{... | collective-permute-start | bytes 36296 | tf_op jit(solution)/shard_map/ppermute | solution.py:20
  33.2 4.0 %collective-permute-start.9 = (f32[42,1]{1,0:T(8,128)}, f32[42,1]{1,0:T(8,128)}, u32[]{:S(2)}, u32[]{:S(2)}) collective-permute-start(f32[42,1]{1,0:T(8,128)} %get-tuple-element.65), channel_id=1, source_target_pairs={{0,8},{8,16},{16,24},{1,9},{9,17},{17,25},{2,10},{10,18},{18,26},{... | collective-permute-start | bytes 512 | tf_op jit(solution)/shard_map/ppermute | solution.py:18
  42.9 3.3 %fusion.2 = f32[3,16,40,128]{3,2,1,0:T(8,128)S(1)} fusion(f32[3,16,40,128]{3,2,1,0:T(8,128)S(1)} %copy.247, f32[4,18,42,1]{3,2,1,0:T(8,128)S(1)} %copy.214, f32[4,18,1,128]{3,2,1,0:T(1,128)S(1)} %copy.211, f32[4,18,1,128]{3,2,1,0:T(1,128)S(1)} %copy.210, f32[4,1,40,128]{3,2,1,0:T(8,128)S(1)} %collective-permute-done.1, ...), kind=kLoop, calls=%fused_computation.18 | loop fusion | flops 10076160 | bytes 4521600 | tf_op jit(solution)/shard_map/add | solution.py:56
  56.4 4.4 %collective-permute-start.10 = (f32[1,128]{1,0:T(1,128)S(1)}, f32[1,128]{1,0:T(1,128)S(1)}, u32[]{:S(2)}, u32[]{:S(2)}) collective-permute-start(f32[1,128]{1,0:T(1,128)S(1)} %get-tuple-element.85), channel_id=1, source_target_pairs={{2,0},{4,2},{6,4},{3,1},{5,3},{7,5},{10,8},{12,10},{14,12},{11,9},... | collective-permute-start | bytes 1544 | tf_op jit(solution)/shard_map/ppermute | solution.py:20
  62.3 4.2 %collective-permute-done.11 = f32[1,128]{1,0:T(1,128)S(1)} collective-permute-done((f32[1,128]{1,0:T(1,128)S(1)}, f32[1,128]{1,0:T(1,128)S(1)}, u32[]{:S(2)}, u32[]{:S(2)}) %collective-permute-start.11) | collective-permute-done | bytes 544 | tf_op jit(solution)/shard_map/ppermute | solution.py:18
  69.3 3.1 %collective-permute-start.13 = (f32[42,1]{1,0:T(8,128)S(1)}, f32[42,1]{1,0:T(8,128)S(1)}, u32[]{:S(2)}, u32[]{:S(2)}) collective-permute-start(f32[42,1]{1,0:T(8,128)S(1)} %get-tuple-element.63), channel_id=1, source_target_pairs={{0,8},{8,16},{16,24},{1,9},{9,17},{17,25},{2,10},{10,18},{18,26},{... | collective-permute-start | bytes 512 | tf_op jit(solution)/shard_map/ppermute | solution.py:18
  72.4 3.5 %collective-permute-done.13 = f32[42,1]{1,0:T(8,128)S(1)} collective-permute-done((f32[42,1]{1,0:T(8,128)S(1)}, f32[42,1]{1,0:T(8,128)S(1)}, u32[]{:S(2)}, u32[]{:S(2)}) %collective-permute-start.13) | collective-permute-done | bytes 200 | tf_op jit(solution)/shard_map/ppermute | solution.py:18
  76.0 3.9 %collective-permute-start.14 = (f32[1,128]{1,0:T(1,128)S(1)}, f32[1,128]{1,0:T(1,128)S(1)}, u32[]{:S(2)}, u32[]{:S(2)}) collective-permute-start(f32[1,128]{1,0:T(1,128)S(1)} %get-tuple-element.83), channel_id=1, source_target_pairs={{2,0},{4,2},{6,4},{3,1},{5,3},{7,5},{10,8},{12,10},{14,12},{11,9},... | collective-permute-start | bytes 1544 | tf_op jit(solution)/shard_map/ppermute | solution.py:20
  81.2 4.2 %collective-permute-done.15 = f32[1,128]{1,0:T(1,128)S(1)} collective-permute-done((f32[1,128]{1,0:T(1,128)S(1)}, f32[1,128]{1,0:T(1,128)S(1)}, u32[]{:S(2)}, u32[]{:S(2)}) %collective-permute-start.15) | collective-permute-done | bytes 544 | tf_op jit(solution)/shard_map/ppermute | solution.py:18
  87.4 3.9 %collective-permute-start.17 = (f32[42,1]{1,0:T(8,128)S(1)}, f32[42,1]{1,0:T(8,128)S(1)}, u32[]{:S(2)}, u32[]{:S(2)}) collective-permute-start(f32[42,1]{1,0:T(8,128)S(1)} %get-tuple-element.61), channel_id=1, source_target_pairs={{0,8},{8,16},{16,24},{1,9},{9,17},{17,25},{2,10},{10,18},{18,26},{... | collective-permute-start | bytes 512 | tf_op jit(solution)/shard_map/ppermute | solution.py:18
  97.8 4.2 %collective-permute-done.19 = f32[1,128]{1,0:T(1,128)S(1)} collective-permute-done((f32[1,128]{1,0:T(1,128)S(1)}, f32[1,128]{1,0:T(1,128)S(1)}, u32[]{:S(2)}, u32[]{:S(2)}) %collective-permute-start.19) | collective-permute-done | bytes 544 | tf_op jit(solution)/shard_map/ppermute | solution.py:18
  104.0 3.9 %collective-permute-start.21 = (f32[42,1]{1,0:T(8,128)S(1)}, f32[42,1]{1,0:T(8,128)S(1)}, u32[]{:S(2)}, u32[]{:S(2)}) collective-permute-start(f32[42,1]{1,0:T(8,128)S(1)} %get-tuple-element.59), channel_id=1, source_target_pairs={{0,8},{8,16},{16,24},{1,9},{9,17},{17,25},{2,10},{10,18},{18,26},{... | collective-permute-start | bytes 512 | tf_op jit(solution)/shard_map/ppermute | solution.py:18
  113.9 4.2 %collective-permute-done.23 = f32[1,128]{1,0:T(1,128)S(1)} collective-permute-done((f32[1,128]{1,0:T(1,128)S(1)}, f32[1,128]{1,0:T(1,128)S(1)}, u32[]{:S(2)}, u32[]{:S(2)}) %collective-permute-start.23) | collective-permute-done | bytes 544 | tf_op jit(solution)/shard_map/ppermute | solution.py:18
  120.1 3.9 %collective-permute-start.25 = (f32[42,1]{1,0:T(8,128)S(1)}, f32[42,1]{1,0:T(8,128)S(1)}, u32[]{:S(2)}, u32[]{:S(2)}) collective-permute-start(f32[42,1]{1,0:T(8,128)S(1)} %get-tuple-element.57), channel_id=1, source_target_pairs={{0,8},{8,16},{16,24},{1,9},{9,17},{17,25},{2,10},{10,18},{18,26},{... | collective-permute-start | bytes 512 | tf_op jit(solution)/shard_map/ppermute | solution.py:18
  130.2 4.2 %collective-permute-done.27 = f32[1,128]{1,0:T(1,128)S(1)} collective-permute-done((f32[1,128]{1,0:T(1,128)S(1)}, f32[1,128]{1,0:T(1,128)S(1)}, u32[]{:S(2)}, u32[]{:S(2)}) %collective-permute-start.27) | collective-permute-done | bytes 544 | tf_op jit(solution)/shard_map/ppermute | solution.py:18
  136.3 3.9 %collective-permute-start.29 = (f32[42,1]{1,0:T(8,128)S(1)}, f32[42,1]{1,0:T(8,128)S(1)}, u32[]{:S(2)}, u32[]{:S(2)}) collective-permute-start(f32[42,1]{1,0:T(8,128)S(1)} %get-tuple-element.55), channel_id=1, source_target_pairs={{0,8},{8,16},{16,24},{1,9},{9,17},{17,25},{2,10},{10,18},{18,26},{... | collective-permute-start | bytes 512 | tf_op jit(solution)/shard_map/ppermute | solution.py:18
  146.3 4.2 %collective-permute-done.31 = f32[1,128]{1,0:T(1,128)S(1)} collective-permute-done((f32[1,128]{1,0:T(1,128)S(1)}, f32[1,128]{1,0:T(1,128)S(1)}, u32[]{:S(2)}, u32[]{:S(2)}) %collective-permute-start.31) | collective-permute-done | bytes 544 | tf_op jit(solution)/shard_map/ppermute | solution.py:18
  152.5 3.9 %collective-permute-start.33 = (f32[42,1]{1,0:T(8,128)S(1)}, f32[42,1]{1,0:T(8,128)S(1)}, u32[]{:S(2)}, u32[]{:S(2)}) collective-permute-start(f32[42,1]{1,0:T(8,128)S(1)} %get-tuple-element.53), channel_id=1, source_target_pairs={{0,8},{8,16},{16,24},{1,9},{9,17},{17,25},{2,10},{10,18},{18,26},{... | collective-permute-start | bytes 512 | tf_op jit(solution)/shard_map/ppermute | solution.py:18
  162.4 4.2 %collective-permute-done.35 = f32[1,128]{1,0:T(1,128)S(1)} collective-permute-done((f32[1,128]{1,0:T(1,128)S(1)}, f32[1,128]{1,0:T(1,128)S(1)}, u32[]{:S(2)}, u32[]{:S(2)}) %collective-permute-start.35) | collective-permute-done | bytes 544 | tf_op jit(solution)/shard_map/ppermute | solution.py:18
  168.6 3.9 %collective-permute-start.37 = (f32[42,1]{1,0:T(8,128)S(1)}, f32[42,1]{1,0:T(8,128)S(1)}, u32[]{:S(2)}, u32[]{:S(2)}) collective-permute-start(f32[42,1]{1,0:T(8,128)S(1)} %get-tuple-element.51), channel_id=1, source_target_pairs={{0,8},{8,16},{16,24},{1,9},{9,17},{17,25},{2,10},{10,18},{18,26},{... | collective-permute-start | bytes 512 | tf_op jit(solution)/shard_map/ppermute | solution.py:18
  178.9 4.2 %collective-permute-done.39 = f32[1,128]{1,0:T(1,128)S(1)} collective-permute-done((f32[1,128]{1,0:T(1,128)S(1)}, f32[1,128]{1,0:T(1,128)S(1)}, u32[]{:S(2)}, u32[]{:S(2)}) %collective-permute-start.39) | collective-permute-done | bytes 544 | tf_op jit(solution)/shard_map/ppermute | solution.py:18
  185.0 4.1 %collective-permute-start.41 = (f32[42,1]{1,0:T(8,128)S(1)}, f32[42,1]{1,0:T(8,128)S(1)}, u32[]{:S(2)}, u32[]{:S(2)}) collective-permute-start(f32[42,1]{1,0:T(8,128)S(1)} %get-tuple-element.49), channel_id=1, source_target_pairs={{0,8},{8,16},{16,24},{1,9},{9,17},{17,25},{2,10},{10,18},{18,26},{... | collective-permute-start | bytes 512 | tf_op jit(solution)/shard_map/ppermute | solution.py:18
  (265 shorter events, 99.9 us)
Async XLA Ops:
  1.9 14.8 %collective-permute-start.6 = (f32[1,128]{1,0:T(1,128)S(1)}, f32[1,128]{1,0:T(1,128)S(1)}, u32[]{:S(2)}, u32[]{:S(2)}) collective-permute-start(f32[1,128]{1,0:T(1,128)S(1)} %broadcast.60), channel_id=1, source_target_pairs={{2,0},{4,2},{6,4},{3,1},{5,3},{7,5},{10,8},{12,10},{14,12},{11,9},... | collective-permute-start | bytes 1544 | tf_op jit(solution)/shard_map/ppermute | solution.py:20
  4.3 12.4 %collective-permute-start.7 = (f32[1,128]{1,0:T(1,128)S(1)}, f32[1,128]{1,0:T(1,128)S(1)}, u32[]{:S(2)}, u32[]{:S(2)}) collective-permute-start(f32[1,128]{1,0:T(1,128)S(1)} %broadcast.60), channel_id=1, source_target_pairs={{0,2},{2,4},{4,6},{1,3},{3,5},{5,7},{8,10},{10,12},{12,14},{9,11},... | collective-permute-start | bytes 1544 | tf_op jit(solution)/shard_map/ppermute | solution.py:18
  10.4 6.4 %collective-permute-start.2 = (f32[4,18,1,128]{3,0,2,1:T(4,128)S(1)}, f32[4,18,1,128]{3,0,2,1:T(4,128)S(1)}, u32[]{:S(2)}, u32[]{:S(2)}) collective-permute-start(f32[4,18,1,128]{3,0,2,1:T(4,128)S(1)} %copy.238), channel_id=1, source_target_pairs={{0,2},{2,4},{4,6},{1,3},{3,5},{5,7},{8,10},{10,12},{12,14},{9,11},... | collective-permute-start | bytes 110600 | tf_op jit(solution)/shard_map/ppermute | solution.py:18
  11.7 6.7 %collective-permute-start.3 = (f32[4,18,1,128]{3,0,2,1:T(4,128)S(1)}, f32[4,18,1,128]{3,0,2,1:T(4,128)S(1)}, u32[]{:S(2)}, u32[]{:S(2)}) collective-permute-start(f32[4,18,1,128]{3,0,2,1:T(4,128)S(1)} %copy.239), channel_id=1, source_target_pairs={{2,0},{4,2},{6,4},{3,1},{5,3},{7,5},{10,8},{12,10},{14,12},{11,9},... | collective-permute-start | bytes 110600 | tf_op jit(solution)/shard_map/ppermute | solution.py:20
  22.6 14.6 %collective-permute-start.4 = (f32[4,18,42,1]{2,0,3,1:T(4,128)S(1)}, f32[4,18,42,1]{2,0,3,1:T(4,128)S(1)}, u32[]{:S(2)}, u32[]{:S(2)}) collective-permute-start(f32[4,18,42,1]{2,0,3,1:T(4,128)S(1)} %copy.212), channel_id=1, source_target_pairs={{0,8},{8,16},{16,24},{1,9},{9,17},{17,25},{2,10},{10,18},{18,26},{... | collective-permute-start | bytes 36296 | tf_op jit(solution)/shard_map/ppermute | solution.py:18
  26.8 11.2 %collective-permute-start.5 = (f32[4,18,42,1]{2,0,3,1:T(4,128)S(1)}, f32[4,18,42,1]{2,0,3,1:T(4,128)S(1)}, u32[]{:S(2)}, u32[]{:S(2)}) collective-permute-start(f32[4,18,42,1]{2,0,3,1:T(4,128)S(1)} %copy.213), channel_id=1, source_target_pairs={{8,0},{16,8},{24,16},{9,1},{17,9},{25,17},{10,2},{18,10},{26,18},{... | collective-permute-start | bytes 36296 | tf_op jit(solution)/shard_map/ppermute | solution.py:20
  30.8 24.7 %collective-permute-start.8 = (f32[42,1]{1,0:T(8,128)}, f32[42,1]{1,0:T(8,128)}, u32[]{:S(2)}, u32[]{:S(2)}) collective-permute-start(f32[42,1]{1,0:T(8,128)} %get-tuple-element.64), channel_id=1, source_target_pairs={{8,0},{16,8},{24,16},{9,1},{17,9},{25,17},{10,2},{18,10},{26,18},{... | collective-permute-start | bytes 512 | tf_op jit(solution)/shard_map/ppermute | solution.py:20
  33.2 22.3 %collective-permute-start.9 = (f32[42,1]{1,0:T(8,128)}, f32[42,1]{1,0:T(8,128)}, u32[]{:S(2)}, u32[]{:S(2)}) collective-permute-start(f32[42,1]{1,0:T(8,128)} %get-tuple-element.65), channel_id=1, source_target_pairs={{0,8},{8,16},{16,24},{1,9},{9,17},{17,25},{2,10},{10,18},{18,26},{... | collective-permute-start | bytes 512 | tf_op jit(solution)/shard_map/ppermute | solution.py:18
  56.4 5.9 %collective-permute-start.10 = (f32[1,128]{1,0:T(1,128)S(1)}, f32[1,128]{1,0:T(1,128)S(1)}, u32[]{:S(2)}, u32[]{:S(2)}) collective-permute-start(f32[1,128]{1,0:T(1,128)S(1)} %get-tuple-element.85), channel_id=1, source_target_pairs={{2,0},{4,2},{6,4},{3,1},{5,3},{7,5},{10,8},{12,10},{14,12},{11,9},... | collective-permute-start | bytes 1544 | tf_op jit(solution)/shard_map/ppermute | solution.py:20
  66.5 5.8 %collective-permute-start.12 = (f32[42,1]{1,0:T(8,128)S(1)}, f32[42,1]{1,0:T(8,128)S(1)}, u32[]{:S(2)}, u32[]{:S(2)}) collective-permute-start(f32[42,1]{1,0:T(8,128)S(1)} %get-tuple-element.62), channel_id=1, source_target_pairs={{8,0},{16,8},{24,16},{9,1},{17,9},{25,17},{10,2},{18,10},{26,18},{... | collective-permute-start | bytes 512 | tf_op jit(solution)/shard_map/ppermute | solution.py:20
  69.3 6.6 %collective-permute-start.13 = (f32[42,1]{1,0:T(8,128)S(1)}, f32[42,1]{1,0:T(8,128)S(1)}, u32[]{:S(2)}, u32[]{:S(2)}) collective-permute-start(f32[42,1]{1,0:T(8,128)S(1)} %get-tuple-element.63), channel_id=1, source_target_pairs={{0,8},{8,16},{16,24},{1,9},{9,17},{17,25},{2,10},{10,18},{18,26},{... | collective-permute-start | bytes 512 | tf_op jit(solution)/shard_map/ppermute | solution.py:18
  85.5 5.8 %collective-permute-start.16 = (f32[42,1]{1,0:T(8,128)S(1)}, f32[42,1]{1,0:T(8,128)S(1)}, u32[]{:S(2)}, u32[]{:S(2)}) collective-permute-start(f32[42,1]{1,0:T(8,128)S(1)} %get-tuple-element.60), channel_id=1, source_target_pairs={{8,0},{16,8},{24,16},{9,1},{17,9},{25,17},{10,2},{18,10},{26,18},{... | collective-permute-start | bytes 512 | tf_op jit(solution)/shard_map/ppermute | solution.py:20
  87.4 6.6 %collective-permute-start.17 = (f32[42,1]{1,0:T(8,128)S(1)}, f32[42,1]{1,0:T(8,128)S(1)}, u32[]{:S(2)}, u32[]{:S(2)}) collective-permute-start(f32[42,1]{1,0:T(8,128)S(1)} %get-tuple-element.61), channel_id=1, source_target_pairs={{0,8},{8,16},{16,24},{1,9},{9,17},{17,25},{2,10},{10,18},{18,26},{... | collective-permute-start | bytes 512 | tf_op jit(solution)/shard_map/ppermute | solution.py:18
  102.0 5.8 %collective-permute-start.20 = (f32[42,1]{1,0:T(8,128)S(1)}, f32[42,1]{1,0:T(8,128)S(1)}, u32[]{:S(2)}, u32[]{:S(2)}) collective-permute-start(f32[42,1]{1,0:T(8,128)S(1)} %get-tuple-element.58), channel_id=1, source_target_pairs={{8,0},{16,8},{24,16},{9,1},{17,9},{25,17},{10,2},{18,10},{26,18},{... | collective-permute-start | bytes 512 | tf_op jit(solution)/shard_map/ppermute | solution.py:20
  104.0 6.6 %collective-permute-start.21 = (f32[42,1]{1,0:T(8,128)S(1)}, f32[42,1]{1,0:T(8,128)S(1)}, u32[]{:S(2)}, u32[]{:S(2)}) collective-permute-start(f32[42,1]{1,0:T(8,128)S(1)} %get-tuple-element.59), channel_id=1, source_target_pairs={{0,8},{8,16},{16,24},{1,9},{9,17},{17,25},{2,10},{10,18},{18,26},{... | collective-permute-start | bytes 512 | tf_op jit(solution)/shard_map/ppermute | solution.py:18
  118.2 5.8 %collective-permute-start.24 = (f32[42,1]{1,0:T(8,128)S(1)}, f32[42,1]{1,0:T(8,128)S(1)}, u32[]{:S(2)}, u32[]{:S(2)}) collective-permute-start(f32[42,1]{1,0:T(8,128)S(1)} %get-tuple-element.56), channel_id=1, source_target_pairs={{8,0},{16,8},{24,16},{9,1},{17,9},{25,17},{10,2},{18,10},{26,18},{... | collective-permute-start | bytes 512 | tf_op jit(solution)/shard_map/ppermute | solution.py:20
  120.1 6.6 %collective-permute-start.25 = (f32[42,1]{1,0:T(8,128)S(1)}, f32[42,1]{1,0:T(8,128)S(1)}, u32[]{:S(2)}, u32[]{:S(2)}) collective-permute-start(f32[42,1]{1,0:T(8,128)S(1)} %get-tuple-element.57), channel_id=1, source_target_pairs={{0,8},{8,16},{16,24},{1,9},{9,17},{17,25},{2,10},{10,18},{18,26},{... | collective-permute-start | bytes 512 | tf_op jit(solution)/shard_map/ppermute | solution.py:18
  134.4 5.8 %collective-permute-start.28 = (f32[42,1]{1,0:T(8,128)S(1)}, f32[42,1]{1,0:T(8,128)S(1)}, u32[]{:S(2)}, u32[]{:S(2)}) collective-permute-start(f32[42,1]{1,0:T(8,128)S(1)} %get-tuple-element.54), channel_id=1, source_target_pairs={{8,0},{16,8},{24,16},{9,1},{17,9},{25,17},{10,2},{18,10},{26,18},{... | collective-permute-start | bytes 512 | tf_op jit(solution)/shard_map/ppermute | solution.py:20
  136.3 6.6 %collective-permute-start.29 = (f32[42,1]{1,0:T(8,128)S(1)}, f32[42,1]{1,0:T(8,128)S(1)}, u32[]{:S(2)}, u32[]{:S(2)}) collective-permute-start(f32[42,1]{1,0:T(8,128)S(1)} %get-tuple-element.55), channel_id=1, source_target_pairs={{0,8},{8,16},{16,24},{1,9},{9,17},{17,25},{2,10},{10,18},{18,26},{... | collective-permute-start | bytes 512 | tf_op jit(solution)/shard_map/ppermute | solution.py:18
  150.5 5.8 %collective-permute-start.32 = (f32[42,1]{1,0:T(8,128)S(1)}, f32[42,1]{1,0:T(8,128)S(1)}, u32[]{:S(2)}, u32[]{:S(2)}) collective-permute-start(f32[42,1]{1,0:T(8,128)S(1)} %get-tuple-element.52), channel_id=1, source_target_pairs={{8,0},{16,8},{24,16},{9,1},{17,9},{25,17},{10,2},{18,10},{26,18},{... | collective-permute-start | bytes 512 | tf_op jit(solution)/shard_map/ppermute | solution.py:20
  152.5 6.6 %collective-permute-start.33 = (f32[42,1]{1,0:T(8,128)S(1)}, f32[42,1]{1,0:T(8,128)S(1)}, u32[]{:S(2)}, u32[]{:S(2)}) collective-permute-start(f32[42,1]{1,0:T(8,128)S(1)} %get-tuple-element.53), channel_id=1, source_target_pairs={{0,8},{8,16},{16,24},{1,9},{9,17},{17,25},{2,10},{10,18},{18,26},{... | collective-permute-start | bytes 512 | tf_op jit(solution)/shard_map/ppermute | solution.py:18
  168.6 6.6 %collective-permute-start.37 = (f32[42,1]{1,0:T(8,128)S(1)}, f32[42,1]{1,0:T(8,128)S(1)}, u32[]{:S(2)}, u32[]{:S(2)}) collective-permute-start(f32[42,1]{1,0:T(8,128)S(1)} %get-tuple-element.51), channel_id=1, source_target_pairs={{0,8},{8,16},{16,24},{1,9},{9,17},{17,25},{2,10},{10,18},{18,26},{... | collective-permute-start | bytes 512 | tf_op jit(solution)/shard_map/ppermute | solution.py:18
  183.1 6.1 %collective-permute-start.40 = (f32[42,1]{1,0:T(8,128)S(1)}, f32[42,1]{1,0:T(8,128)S(1)}, u32[]{:S(2)}, u32[]{:S(2)}) collective-permute-start(f32[42,1]{1,0:T(8,128)S(1)} %get-tuple-element.48), channel_id=1, source_target_pairs={{8,0},{16,8},{24,16},{9,1},{17,9},{25,17},{10,2},{18,10},{26,18},{... | collective-permute-start | bytes 512 | tf_op jit(solution)/shard_map/ppermute | solution.py:20
  185.0 6.6 %collective-permute-start.41 = (f32[42,1]{1,0:T(8,128)S(1)}, f32[42,1]{1,0:T(8,128)S(1)}, u32[]{:S(2)}, u32[]{:S(2)}) collective-permute-start(f32[42,1]{1,0:T(8,128)S(1)} %get-tuple-element.49), channel_id=1, source_target_pairs={{0,8},{8,16},{16,24},{1,9},{9,17},{17,25},{2,10},{10,18},{18,26},{... | collective-permute-start | bytes 512 | tf_op jit(solution)/shard_map/ppermute | solution.py:18
  (73 other events, 952.4 us)
